TPU v7x, 256 devices: a whole 4x4x8 slice. The times are simulated.
256 devices in a mesh: grp: 8 (over z_hi, core), mem: 32 (over z_lo, x, y).
Axes of the slice: x: 4, y: 4, z: 8 (z_hi: 4, z_lo: 2; z = z_hi * 2 + z_lo), core: 2. Of those that a mesh axis runs over, the one named last changes fastest.
Arguments:
- spectra: bfloat16 [2048, 2, 16, 512], P(('grp', 'mem')), may hold values from -40 to 40
- partners: int32 [2, 32], replicated, may hold values from 0 to 7, as said below
Outputs:
- correlations: bfloat16 [2048, 2, 256, 513], P(('grp', 'mem'))
Inputs may be any that keep to these rules, and one draw needn't show every extreme that they name: For each member index k the offsets partners[r, k] of the rounds are distinct (offset 0 pairs a block with its own group).
All inputs are finite; a program needn't handle non-finite values.
Results may differ from a plain program's by a relative error of at most 0.0068.
Values may be sent and summed in bfloat16 or wider, within the bound.
No kernel may reach another device: no remote copies, remote signals or barrier semaphores. Data moves between devices by JAX's collectives and lax.ppermute only.
A program may use at most 128 MiB of HBM per device.

v0:
```python
import math
import jax
import jax.numpy as jnp
from jax import lax
from jax.sharding import PartitionSpec as P

SMOOTH = 32


def from_partner(array, axis, distance):
    return lax.ppermute(array, axis, [(i, i ^ 1 << distance) for i in range(lax.axis_size(axis))])


def whiten(spectra, half_width):
    components = spectra.astype(jnp.float32)
    power_sum = components[:, 0] * components[:, 0] + components[:, 1] * components[:, 1]
    bin_count = power_sum.shape[-1]
    positions = jnp.arange(bin_count, dtype=jnp.int32)
    band_matrix = (jnp.abs(positions[:, None] - positions[None, :]) <= half_width).astype(
        jnp.float32
    )
    smooth = jnp.dot(power_sum.reshape(-1, bin_count), band_matrix, precision=lax.Precision.HIGHEST)
    smooth = smooth.reshape(power_sum.shape) / (2 * half_width + 1)
    inv_level = lax.rsqrt(smooth + 1e-05)
    return (components * inv_level[:, None]).astype(jnp.bfloat16)


def lag_table(bin_count):
    centre = bin_count // 2
    frequency = jnp.arange(bin_count, dtype=jnp.int32)[:, None]
    lag_offset = jnp.arange(bin_count + 1, dtype=jnp.int32)[None, :] - centre
    angles = jnp.mod(frequency * lag_offset, 2 * bin_count).astype(jnp.float32) * (
        math.pi / bin_count
    )
    return jnp.stack([jnp.cos(angles), -jnp.sin(angles)], 0).astype(jnp.bfloat16)


def pair_lags(own_block, partner_block, transform):
    factor = math.sqrt(2.0 / (own_block.shape[3] * own_block.shape[2]))
    rotated = jnp.stack([own_block, jnp.stack([own_block[:, 1], -own_block[:, 0]], 1)], 0)
    cross_spectra = jnp.einsum(
        "oicsf,jcsf->ofij", rotated, partner_block, preferred_element_type=jnp.float32
    ).astype(jnp.bfloat16)
    lag_sums = jnp.einsum(
        "ofij,ofl->ijl", cross_spectra, transform, preferred_element_type=jnp.float32
    )
    return (lag_sums * factor).astype(jnp.bfloat16)


def correlate_piece(own_block, transform, received):
    return pair_lags(own_block, received, transform)


def route_shard(payload, offset, levels):
    for level in range(levels):
        swapped = from_partner(payload, "grp", level)
        payload = jnp.where(offset // 2**level % 2 == 1, swapped, payload)
    return payload


def on_device(spectra, partners):
    whitened = whiten(spectra, SMOOTH)
    transform = lag_table(spectra.shape[3])
    rounds = partners.shape[0]
    member_index = lax.axis_index("mem")
    levels = lax.axis_size("grp").bit_length() - 1
    outputs = []
    for round_index in range(rounds):
        own_offset = partners[round_index, member_index]
        source = route_shard(whitened, own_offset, levels)
        outputs.append(
            correlate_piece(whitened, transform, lax.all_gather(source, "mem", axis=0, tiled=True))
        )
    return jnp.stack(outputs, 1)


def solution(mesh):
    placed = (P(("grp", "mem"), None, None, None), P())
    return jax.shard_map(
        on_device,
        mesh=mesh,
        in_specs=placed,
        out_specs=P(("grp", "mem"), None, None, None),
        check_vma=False,
    )
```

profile of v0, /device:TPU:8, one launch (start us, length us, event | category | flops | bytes accessed | tf_op | source)
XLA Modules:
  0.0 450.0 jit_solution(15983893650686171145)
XLA Ops:
  6.5 1.0 convert_element_type.42
  8.0 1.0 multiply_convert_fusion
  9.1 1.3 constant_dynamic-slice_fusion.1
  14.2 1.1 broadcast_select_fusion.3
  15.2 3.4 collective-permute-start.1
  19.3 11.9 %collective-permute-done.1 = bf16[8,2,16,512]{3,2,1,0:T(8,128)(2,1)S(1)} collective-permute-done((bf16[8,2,16,512]{3,2,1,0:T(8,128)(2,1)S(1)}, bf16[8,2,16,512]{3,2,1,0:T(8,128)(2,1)S(1)}, u32[]{:S(2)}, u32[]{:S(2)}) %collective-permute-start.1) | collective-permute-done | bytes 262176 | tf_op jit(solution)/shard_map/ppermute | solution.py:11
  31.2 6.6 %collective-permute-start.2 = (bf16[8,2,16,512]{3,2,1,0:T(8,128)(2,1)S(1)}, bf16[8,2,16,512]{3,2,1,0:T(8,128)(2,1)S(1)}, u32[]{:S(2)}, u32[]{:S(2)}) collective-permute-start(bf16[8,2,16,512]{3,2,1,0:T(8,128)(2,1)S(1)} %broadcast_select_fusion.4), channel_id=1, source_target_pairs={{0,128},{32,160},{64,192},{96,224},{128,0},{160,32},{192,64},{224,... | collective-permute-start | bytes 786440 | tf_op jit(solution)/shard_map/ppermute | solution.py:11
  37.9 11.9 %collective-permute-done.2 = bf16[8,2,16,512]{3,2,1,0:T(8,128)(2,1)S(1)} collective-permute-done((bf16[8,2,16,512]{3,2,1,0:T(8,128)(2,1)S(1)}, bf16[8,2,16,512]{3,2,1,0:T(8,128)(2,1)S(1)}, u32[]{:S(2)}, u32[]{:S(2)}) %collective-permute-start.2) | collective-permute-done | bytes 262176 | tf_op jit(solution)/shard_map/ppermute | solution.py:11
  49.7 0.7 broadcast_select_fusion.5
  51.2 10.8 %collective-permute-done.3 = bf16[8,2,16,512]{3,2,1,0:T(8,128)(2,1)S(1)} collective-permute-done((bf16[8,2,16,512]{3,2,1,0:T(8,128)(2,1)S(1)}, bf16[8,2,16,512]{3,2,1,0:T(8,128)(2,1)S(1)}, u32[]{:S(2)}, u32[]{:S(2)}) %collective-permute-start.3) | collective-permute-done | bytes 262176 | tf_op jit(solution)/shard_map/ppermute | solution.py:11
  62.1 5.1 %collective-permute-start.4 = (bf16[8,2,16,512]{3,2,1,0:T(8,128)(2,1)S(1)}, bf16[8,2,16,512]{3,2,1,0:T(8,128)(2,1)S(1)}, u32[]{:S(2)}, u32[]{:S(2)}) collective-permute-start(bf16[8,2,16,512]{3,2,1,0:T(8,128)(2,1)S(1)} %broadcast_select_fusion.1), channel_id=1, source_target_pairs={{0,128},{32,160},{64,192},{96,224},{128,0},{160,32},{192,64},{224,... | collective-permute-start | bytes 786440 | tf_op jit(solution)/shard_map/ppermute | solution.py:11
  67.2 11.3 %collective-permute-done.4 = bf16[8,2,16,512]{3,2,1,0:T(8,128)(2,1)S(1)} collective-permute-done((bf16[8,2,16,512]{3,2,1,0:T(8,128)(2,1)S(1)}, bf16[8,2,16,512]{3,2,1,0:T(8,128)(2,1)S(1)}, u32[]{:S(2)}, u32[]{:S(2)}) %collective-permute-start.4) | collective-permute-done | bytes 262176 | tf_op jit(solution)/shard_map/ppermute | solution.py:11
  78.5 0.7 broadcast_select_fusion.2
  79.4 6.4 %copy.6 = bf16[2,8,2,16,512]{3,1,2,0,4:T(8,128)(2,1)} copy(bf16[2,8,2,16,512]{4,3,2,1,0:T(8,128)(2,1)S(1)} %pad_maximum_fusion.1) | data formatting | bytes 1048576 | tf_op jit(solution)/shard_map/stack | solution.py:40
  85.9 4.7 %cosine_convert_fusion = (bf16[1,512,513]{1,2,0:T(8,128)(2,1)S(1)}, bf16[1,512,513]{1,2,0:T(8,128)(2,1)S(1)}) fusion(s32[513]{0:T(1024)S(1)} %iota_add_fusion), kind=kLoop, calls=%fused_computation.24 | loop fusion | flops 4465152 | bytes 1052676 | tf_op jit(solution)/shard_map/convert
  90.6 132.0 %all-gather.3.cloned.1.call-done = bf16[256,2,16,512]{3,2,1,0:T(8,128)(2,1)} async-done(((bf16[8,2,16,512]{3,2,1,0:T(8,128)(2,1)}), bf16[256,2,16,512]{3,2,1,0:T(8,128)(2,1)}) %all-gather.3.cloned.1.call-update) | async-done | bytes 8388624 | tf_op jit(solution)/shard_map/all_gather | solution.py:72
  222.6 15.9 %copy.5 = bf16[256,2,16,512,1]{0,2,1,4,3:T(8,128)(2,1)} copy(bf16[256,2,16,512,1]{3,2,1,0,4:T(8,128)(2,1)} %bitcast.64) | data formatting | bytes 16777216 | tf_op jit(solution)/shard_map/all_gather | solution.py:72
  238.6 158.3 %all-gather.5.cloned.1.call-done = bf16[256,2,16,512]{3,2,1,0:T(8,128)(2,1)} async-done(((bf16[8,2,16,512]{3,2,1,0:T(8,128)(2,1)}), bf16[256,2,16,512]{3,2,1,0:T(8,128)(2,1)}) %all-gather.5.cloned.1.call-update) | async-done | bytes 8388624 | tf_op jit(solution)/shard_map/all_gather | solution.py:72
  396.9 16.0 %copy.9 = bf16[256,2,16,512,1]{0,2,1,4,3:T(8,128)(2,1)} copy(bf16[256,2,16,512,1]{3,2,1,0,4:T(8,128)(2,1)} %bitcast.65) | data formatting | bytes 16777216 | tf_op jit(solution)/shard_map/all_gather | solution.py:72
  412.9 8.0 %fusion.32 = bf16[512,256,2,8,1]{1,3,4,2,0:T(8,128)(2,1)} fusion(bf16[256,2,16,512,1]{0,2,1,4,3:T(8,128)(2,1)} %copy.5, bf16[2,8,2,16,512]{3,1,2,0,4:T(8,128)(2,1)} %copy.6), kind=kOutput, calls=%fused_computation.52 | convolution fusion | flops 134217728 | bytes 13107200 | tf_op jit(solution)/shard_map/oicsf,jcsf->ofij/dot_general | solution.py:41
  420.8 7.9 %fusion.33 = bf16[512,256,2,8,1]{1,3,4,2,0:T(8,128)(2,1)} fusion(bf16[256,2,16,512,1]{0,2,1,4,3:T(8,128)(2,1)} %copy.9, bf16[2,8,2,16,512]{3,1,2,0,4:T(8,128)(2,1)} %copy.6), kind=kOutput, calls=%fused_computation.53 | convolution fusion | flops 134217728 | bytes 13107200 | tf_op jit(solution)/shard_map/oicsf,jcsf->ofij/dot_general | solution.py:41
  428.8 5.0 %fusion.8 = bf16[8,1,256,513]{2,3,0,1:T(8,128)(2,1)S(1)} fusion(bf16[512,256,2,8,1]{1,3,4,2,0:T(8,128)(2,1)} %fusion.32, bf16[1,512,513]{1,2,0:T(8,128)(2,1)S(1)} %get-tuple-element.10, bf16[1,512,513]{1,2,0:T(8,128)(2,1)S(1)} %get-tuple-element.9), kind=kOutput, calls=%fused_computation.11 | convolution fusion | flops 2154304512 | bytes 7346176 | tf_op jit(solution)/shard_map/ofij,ofl->ijl/dot_general | solution.py:44
  433.8 2.7 fusion.9
  436.8 6.3 %copy.4 = bf16[8,2,256,513]{2,1,3,0:T(2,128)(2,1)} copy(bf16[8,2,256,513]{2,3,0,1:T(8,128)(2,1)S(1)} %pad_maximum_fusion) | data formatting | bytes 8404992 | tf_op jit(solution)/shard_map/stack | solution.py:74
  (20 shorter events, 1.3 us)
Async XLA Ops:
  6.5 216.1 %all-gather.3.cloned.1.call-start = ((), (), s32[]{:S(2)}) async-start(), calls=%async_computation | async-start | bytes 8650752 | tf_op jit(solution)/shard_map/all_gather | solution.py:72
  7.5 71.8 %copy-start = (bf16[8,2,16,512]{3,2,1,0:T(8,128)(2,1)S(1)}, bf16[8,2,16,512]{3,2,1,0:T(8,128)(2,1)}, u32[]{:S(2)}) copy-start(bf16[8,2,16,512]{3,2,1,0:T(8,128)(2,1)} %param.2) | copy-start | bytes 786436
  9.0 5.1 %collective-permute-start = (bf16[8,2,16,512]{3,2,1,0:T(8,128)(2,1)S(1)}, bf16[8,2,16,512]{3,2,1,0:T(8,128)(2,1)S(1)}, u32[]{:S(2)}, u32[]{:S(2)}) collective-permute-start(bf16[8,2,16,512]{3,2,1,0:T(8,128)(2,1)S(1)} %multiply_convert_fusion), channel_id=1, source_target_pairs={{0,32},{32,0},{64,96},{96,64},{128,160},{160,128},{192,224},{224,1... | collective-permute-start | bytes 786440 | tf_op jit(solution)/shard_map/ppermute | solution.py:11
  15.2 15.9 %collective-permute-start.1 = (bf16[8,2,16,512]{3,2,1,0:T(8,128)(2,1)S(1)}, bf16[8,2,16,512]{3,2,1,0:T(8,128)(2,1)S(1)}, u32[]{:S(2)}, u32[]{:S(2)}) collective-permute-start(bf16[8,2,16,512]{3,2,1,0:T(8,128)(2,1)S(1)} %get-tuple-element.5), channel_id=1, source_target_pairs={{0,64},{32,96},{64,0},{96,32},{128,192},{160,224},{192,128},{224,1... | collective-permute-start | bytes 786440 | tf_op jit(solution)/shard_map/ppermute | solution.py:11
  31.2 18.5 %collective-permute-start.2 = (bf16[8,2,16,512]{3,2,1,0:T(8,128)(2,1)S(1)}, bf16[8,2,16,512]{3,2,1,0:T(8,128)(2,1)S(1)}, u32[]{:S(2)}, u32[]{:S(2)}) collective-permute-start(bf16[8,2,16,512]{3,2,1,0:T(8,128)(2,1)S(1)} %broadcast_select_fusion.4), channel_id=1, source_target_pairs={{0,128},{32,160},{64,192},{96,224},{128,0},{160,32},{192,64},{224,... | collective-permute-start | bytes 786440 | tf_op jit(solution)/shard_map/ppermute | solution.py:11
  50.5 346.4 %all-gather.5.cloned.1.call-start = ((), (), s32[]{:S(2)}) async-start(), calls=%async_computation.1 | async-start | bytes 8650752 | tf_op jit(solution)/shard_map/all_gather | solution.py:72
  50.5 11.5 %collective-permute-start.3 = (bf16[8,2,16,512]{3,2,1,0:T(8,128)(2,1)S(1)}, bf16[8,2,16,512]{3,2,1,0:T(8,128)(2,1)S(1)}, u32[]{:S(2)}, u32[]{:S(2)}) collective-permute-start(bf16[8,2,16,512]{3,2,1,0:T(8,128)(2,1)S(1)} %get-tuple-element.6), channel_id=1, source_target_pairs={{0,64},{32,96},{64,0},{96,32},{128,192},{160,224},{192,128},{224,1... | collective-permute-start | bytes 786440 | tf_op jit(solution)/shard_map/ppermute | solution.py:11
  62.1 16.4 %collective-permute-start.4 = (bf16[8,2,16,512]{3,2,1,0:T(8,128)(2,1)S(1)}, bf16[8,2,16,512]{3,2,1,0:T(8,128)(2,1)S(1)}, u32[]{:S(2)}, u32[]{:S(2)}) collective-permute-start(bf16[8,2,16,512]{3,2,1,0:T(8,128)(2,1)S(1)} %broadcast_select_fusion.1), channel_id=1, source_target_pairs={{0,128},{32,160},{64,192},{96,224},{128,0},{160,32},{192,64},{224,... | collective-permute-start | bytes 786440 | tf_op jit(solution)/shard_map/ppermute | solution.py:11
  428.8 5.0 %copy-start.1 = (bf16[512,256,2,8,1]{1,3,4,2,0:T(8,128)(2,1)S(1)}, bf16[512,256,2,8,1]{1,3,4,2,0:T(8,128)(2,1)}, u32[]{:S(2)}) copy-start(bf16[512,256,2,8,1]{1,3,4,2,0:T(8,128)(2,1)} %fusion.33) | copy-start | bytes 12582916
Sparse Core Ops, SparseCore 0:
  50.6 171.9 all-gather.2
  224.4 172.4 all-gather.4
where the time goes:
time: 451 us; the launch traced here: 450 us
  waiting for transfers between devices  336 us (75%)
  local copies, waits for them, and re-layouts  46 us (10%)
  matrix products  24 us (5%)
  between operations  18.5 us (4%)
  starting transfers between devices  15.3 us (3%)
  other arithmetic  9.86 us (2%)
    all_gather x2, waiting for transfers between devices, on_device(): lax.all_gather(source, 'mem', axis=0, tiled=True)  290 us
    ppermute x5, waiting for transfers between devices, from_partner(): lax.ppermute(array, axis, [(i, i ^ 1 << distance) for i in range(lax.axis...  45.9 us
    all_gather x2, local copies, waits for them, and re-layouts, on_device(): lax.all_gather(source, 'mem', axis=0, tiled=True)  31.9 us
    dot_general x2, matrix products, pair_lags(): jnp.einsum('oicsf,jcsf->ofij', rotated, partner_block, preferred_element_...  15.9 us
    ppermute x5, starting transfers between devices, from_partner(): lax.ppermute(array, axis, [(i, i ^ 1 << distance) for i in range(lax.axis...  15.3 us
  transfers between devices with their start and end apart: 7, of which 6 were waited for; matrix products, arithmetic and copies ran while one was open for 7% of the time, Pallas kernels for 0%

commit v1 on v0

--- a/solution.py
+++ b/solution.py
@@ -3,6 +3,7 @@
 import jax.numpy as jnp
 from jax import lax
 from jax.sharding import PartitionSpec as P
+from jax.lax import all_to_all, axis_size
 
 SMOOTH = 32
 
@@ -68,9 +69,15 @@
     for round_index in range(rounds):
         own_offset = partners[round_index, member_index]
         source = route_shard(whitened, own_offset, levels)
-        outputs.append(
-            correlate_piece(whitened, transform, lax.all_gather(source, "mem", axis=0, tiled=True))
-        )
+
+        def review_the_scenes(x_in, device_axis):
+            block_next = jnp.concatenate(
+                all_to_all(jnp.stack([x_in] * axis_size(device_axis), axis=0), device_axis, 0, 0),
+                axis=0,
+            )
+            return block_next
+
+        outputs.append(correlate_piece(whitened, transform, review_the_scenes(source, "mem")))
     return jnp.stack(outputs, 1)
 
 

time: 451 us -> 379 us (0.84)
  waiting for transfers between devices: 336 us -> 222 us
  starting transfers between devices: 15.3 us -> 60.1 us
  between operations: 18.5 us -> 5.39 us
  local copies, waits for them, and re-layouts: 46 us -> 54.7 us
    all_gather x2 -> x0, waiting for transfers between devices: 290 us -> none  [on_device(): lax.all_gather(source, 'mem', axis=0, tiled=True)]
    all_to_all x0 -> x2, waiting for transfers between devices: none -> 92.7 us  [review_the_scenes(): all_to_all(jnp.stack([x_in] * axis_size(device_axis), axis=0), device_axi...]
    ppermute x5, waiting for transfers between devices: 45.9 us -> 129 us  [from_partner(): lax.ppermute(array, axis, [(i, i ^ 1 << distance) for i in range(lax.axis...]
    all_gather x2 -> x0, local copies, waits for them, and re-layouts: 31.9 us -> none  [on_device(): lax.all_gather(source, 'mem', axis=0, tiled=True)]
    reshape x0 -> x2, local copies, waits for them, and re-layouts: none -> 31.9 us  [review_the_scenes(): jnp.concatenate(all_to_all(jnp.stack([x_in] * axis_size(device_axis), axi...]
    all_to_all x0 -> x2, starting transfers between devices: none -> 28.6 us  [review_the_scenes(): all_to_all(jnp.stack([x_in] * axis_size(device_axis), axis=0), device_axi...]
    ppermute x5, starting transfers between devices: 15.3 us -> 31.5 us  [from_partner(): lax.ppermute(array, axis, [(i, i ^ 1 << distance) for i in range(lax.axis...]
    another operation x0 -> x2, local copies, waits for them, and re-layouts: none -> 8.6 us  [review_the_scenes(): jnp.stack([x_in] * axis_size(device_axis), axis=0)]
  transfers between devices with their start and end apart: 7 -> 7, of which waited for: 6 -> 5; matrix products, arithmetic and copies ran while one was open for 7% -> 8% of each run, Pallas kernels for 0% -> 0%
where the time goes in v1:
time: 379 us; the launch traced here: 375 us
  waiting for transfers between devices  222 us (59%)
  starting transfers between devices  60.1 us (16%)
  local copies, waits for them, and re-layouts  54.7 us (14%)
  matrix products  24 us (6%)
  other arithmetic  8.45 us (2%)
  between operations  5.39 us (1%)
    ppermute x5, waiting for transfers between devices, from_partner(): lax.ppermute(array, axis, [(i, i ^ 1 << distance) for i in range(lax.axis...  129 us
    all_to_all x2, waiting for transfers between devices, review_the_scenes(): all_to_all(jnp.stack([x_in] * axis_size(device_axis), axis=0), device_axi...  92.7 us
    reshape x2, local copies, waits for them, and re-layouts, review_the_scenes(): jnp.concatenate(all_to_all(jnp.stack([x_in] * axis_size(device_axis), axi...  31.9 us
    ppermute x5, starting transfers between devices, from_partner(): lax.ppermute(array, axis, [(i, i ^ 1 << distance) for i in range(lax.axis...  31.5 us
    all_to_all x2, starting transfers between devices, review_the_scenes(): all_to_all(jnp.stack([x_in] * axis_size(device_axis), axis=0), device_axi...  28.6 us
    dot_general x2, matrix products, pair_lags(): jnp.einsum('oicsf,jcsf->ofij', rotated, partner_block, preferred_element_...  15.9 us
    another operation x2, local copies, waits for them, and re-layouts, review_the_scenes(): jnp.stack([x_in] * axis_size(device_axis), axis=0)  8.6 us
    dot_general x2, matrix products, pair_lags(): jnp.einsum('ofij,ofl->ijl', cross_spectra, transform, preferred_element_t...  7.68 us
  transfers between devices with their start and end apart: 7, of which 5 were waited for; matrix products, arithmetic and copies ran while one was open for 8% of the time, Pallas kernels for 0%

profile of v1, /device:TPU:8, one launch (start us, length us, event | category | flops | bytes accessed | tf_op | source)
XLA Modules:
  0.0 374.8 jit_solution(12017292306454810374)
XLA Ops:
  2.6 1.4 constant_dynamic-slice_fusion.1
  7.8 1.1 broadcast_select_fusion.3
  8.9 3.4 collective-permute-start.3
  12.9 11.9 %collective-permute-done.3 = bf16[8,2,16,512]{3,2,1,0:T(8,128)(2,1)S(1)} collective-permute-done((bf16[8,2,16,512]{3,2,1,0:T(8,128)(2,1)S(1)}, bf16[8,2,16,512]{3,2,1,0:T(8,128)(2,1)S(1)}, u32[]{:S(2)}, u32[]{:S(2)}) %collective-permute-start.3) | collective-permute-done | bytes 262176 | tf_op jit(solution)/shard_map/ppermute | solution.py:12
  24.9 6.6 %collective-permute-start.4 = (bf16[8,2,16,512]{3,2,1,0:T(8,128)(2,1)S(1)}, bf16[8,2,16,512]{3,2,1,0:T(8,128)(2,1)S(1)}, u32[]{:S(2)}, u32[]{:S(2)}) collective-permute-start(bf16[8,2,16,512]{3,2,1,0:T(8,128)(2,1)S(1)} %broadcast_select_fusion.1), channel_id=1, source_target_pairs={{0,128},{32,160},{64,192},{96,224},{128,0},{160,32},{192,64},{224,... | collective-permute-start | bytes 786440 | tf_op jit(solution)/shard_map/ppermute | solution.py:12
  31.5 11.9 %collective-permute-done.4 = bf16[8,2,16,512]{3,2,1,0:T(8,128)(2,1)S(1)} collective-permute-done((bf16[8,2,16,512]{3,2,1,0:T(8,128)(2,1)S(1)}, bf16[8,2,16,512]{3,2,1,0:T(8,128)(2,1)S(1)}, u32[]{:S(2)}, u32[]{:S(2)}) %collective-permute-start.4) | collective-permute-done | bytes 262176 | tf_op jit(solution)/shard_map/ppermute | solution.py:12
  43.4 4.3 %stack.28 = bf16[32,8,2,16,512]{4,3,2,1,0:T(8,128)(2,1)} broadcast(bf16[8,2,16,512]{3,2,1,0:T(8,128)(2,1)S(1)} %broadcast_select_fusion.2), dimensions={1,2,3,4} | broadcast | bytes 8650752 | tf_op jit(solution)/shard_map/stack | solution.py:75
  47.7 7.6 %all-to-all-start.1 = ((bf16[32,8,2,16,512]{4,3,2,1,0:T(8,128)(2,1)}), bf16[32,8,2,16,512]{4,3,2,1,0:T(8,128)(2,1)}, u32[]{:S(2)}, u32[]{:S(2)}) async-start(bf16[32,8,2,16,512]{4,3,2,1,0:T(8,128)(2,1)} %stack.28), calls=%async_computation.1 | async-start | bytes 16777216 | tf_op jit(solution)/shard_map/all_to_all | solution.py:75
  55.3 3.1 collective-permute-start.1
  59.1 101.0 %collective-permute-done.1 = bf16[8,2,16,512]{3,2,1,0:T(8,128)(2,1)S(1)} collective-permute-done((bf16[8,2,16,512]{3,2,1,0:T(8,128)(2,1)S(1)}, bf16[8,2,16,512]{3,2,1,0:T(8,128)(2,1)S(1)}, u32[]{:S(2)}, u32[]{:S(2)}) %collective-permute-start.1) | collective-permute-done | bytes 262176 | tf_op jit(solution)/shard_map/ppermute | solution.py:12
  160.1 18.3 %collective-permute-start.2 = (bf16[8,2,16,512]{3,2,1,0:T(8,128)(2,1)S(1)}, bf16[8,2,16,512]{3,2,1,0:T(8,128)(2,1)S(1)}, u32[]{:S(2)}, u32[]{:S(2)}) collective-permute-start(bf16[8,2,16,512]{3,2,1,0:T(8,128)(2,1)S(1)} %broadcast_select_fusion.4), channel_id=1, source_target_pairs={{0,128},{32,160},{64,192},{96,224},{128,0},{160,32},{192,64},{224,... | collective-permute-start | bytes 786440 | tf_op jit(solution)/shard_map/ppermute | solution.py:12
  178.5 4.7 %collective-permute-done.2 = bf16[8,2,16,512]{3,2,1,0:T(8,128)(2,1)S(1)} collective-permute-done((bf16[8,2,16,512]{3,2,1,0:T(8,128)(2,1)S(1)}, bf16[8,2,16,512]{3,2,1,0:T(8,128)(2,1)S(1)}, u32[]{:S(2)}, u32[]{:S(2)}) %collective-permute-start.2) | collective-permute-done | bytes 262176 | tf_op jit(solution)/shard_map/ppermute | solution.py:12
  183.2 4.3 %stack.21 = bf16[32,8,2,16,512]{4,3,2,1,0:T(8,128)(2,1)} broadcast(bf16[8,2,16,512]{3,2,1,0:T(8,128)(2,1)S(1)} %broadcast_select_fusion.5), dimensions={1,2,3,4} | broadcast | bytes 8650752 | tf_op jit(solution)/shard_map/stack | solution.py:75
  187.5 21.0 %all-to-all-start = ((bf16[32,8,2,16,512]{4,3,2,1,0:T(8,128)(2,1)}), bf16[32,8,2,16,512]{4,3,2,1,0:T(8,128)(2,1)}, u32[]{:S(2)}, u32[]{:S(2)}) async-start(bf16[32,8,2,16,512]{4,3,2,1,0:T(8,128)(2,1)} %stack.21), calls=%async_computation | async-start | bytes 16777216 | tf_op jit(solution)/shard_map/all_to_all | solution.py:75
  208.7 6.4 %copy.5 = bf16[2,8,2,16,512]{3,1,2,0,4:T(8,128)(2,1)} copy(bf16[2,8,2,16,512]{4,3,2,1,0:T(8,128)(2,1)S(1)} %pad_maximum_fusion.1) | data formatting | bytes 1048576 | tf_op jit(solution)/shard_map/stack | solution.py:41
  215.2 4.7 %cosine_convert_fusion = (bf16[1,512,513]{1,2,0:T(8,128)(2,1)S(1)}, bf16[1,512,513]{1,2,0:T(8,128)(2,1)S(1)}) fusion(s32[513]{0:T(1024)S(1)} %iota_add_fusion), kind=kLoop, calls=%fused_computation.24 | loop fusion | flops 4465152 | bytes 1052676 | tf_op jit(solution)/shard_map/convert
  219.9 16.0 %copy.8 = bf16[256,2,16,512,1]{0,2,1,4,3:T(8,128)(2,1)} copy(bf16[256,2,16,512,1]{3,2,1,0,4:T(8,128)(2,1)} %bitcast.15) | data formatting | bytes 16777216 | tf_op jit(solution)/shard_map/reshape | solution.py:74
  235.9 92.7 %all-to-all-done = bf16[32,8,2,16,512]{4,3,2,1,0:T(8,128)(2,1)} async-done(((bf16[32,8,2,16,512]{4,3,2,1,0:T(8,128)(2,1)}), bf16[32,8,2,16,512]{4,3,2,1,0:T(8,128)(2,1)}, u32[]{:S(2)}, u32[]{:S(2)}) %all-to-all-start) | async-done | bytes 8388640 | tf_op jit(solution)/shard_map/all_to_all | solution.py:75
  328.6 15.9 %copy.4 = bf16[256,2,16,512,1]{0,2,1,4,3:T(8,128)(2,1)} copy(bf16[256,2,16,512,1]{3,2,1,0,4:T(8,128)(2,1)} %bitcast.4) | data formatting | bytes 16777216 | tf_op jit(solution)/shard_map/reshape | solution.py:74
  344.5 8.0 %fusion.33 = bf16[512,256,2,8,1]{1,3,4,2,0:T(8,128)(2,1)} fusion(bf16[256,2,16,512,1]{0,2,1,4,3:T(8,128)(2,1)} %copy.8, bf16[2,8,2,16,512]{3,1,2,0,4:T(8,128)(2,1)} %copy.5), kind=kOutput, calls=%fused_computation.53 | convolution fusion | flops 134217728 | bytes 13107200 | tf_op jit(solution)/shard_map/oicsf,jcsf->ofij/dot_general | solution.py:42
  352.4 7.9 %fusion.32 = bf16[512,256,2,8,1]{1,3,4,2,0:T(8,128)(2,1)} fusion(bf16[256,2,16,512,1]{0,2,1,4,3:T(8,128)(2,1)} %copy.4, bf16[2,8,2,16,512]{3,1,2,0,4:T(8,128)(2,1)} %copy.5), kind=kOutput, calls=%fused_computation.52 | convolution fusion | flops 134217728 | bytes 13107200 | tf_op jit(solution)/shard_map/oicsf,jcsf->ofij/dot_general | solution.py:42
  360.4 5.0 %fusion.9 = bf16[8,1,256,513]{2,3,0,1:T(8,128)(2,1)S(1)} fusion(bf16[512,256,2,8,1]{1,3,4,2,0:T(8,128)(2,1)} %fusion.33, bf16[1,512,513]{1,2,0:T(8,128)(2,1)S(1)} %get-tuple-element.10, bf16[1,512,513]{1,2,0:T(8,128)(2,1)S(1)} %get-tuple-element.9), kind=kOutput, calls=%fused_computation.12 | convolution fusion | flops 2154304512 | bytes 7346176 | tf_op jit(solution)/shard_map/ofij,ofl->ijl/dot_general | solution.py:45
  365.4 2.7 fusion.8
  368.4 6.3 %copy.3 = bf16[8,2,256,513]{2,1,3,0:T(2,128)(2,1)} copy(bf16[8,2,256,513]{2,3,0,1:T(8,128)(2,1)S(1)} %pad_maximum_fusion) | data formatting | bytes 8404992 | tf_op jit(solution)/shard_map/stack | solution.py:81
  (20 shorter events, 3.2 us)
Async XLA Ops:
  2.5 5.3 %collective-permute-start = (bf16[8,2,16,512]{3,2,1,0:T(8,128)(2,1)S(1)}, bf16[8,2,16,512]{3,2,1,0:T(8,128)(2,1)S(1)}, u32[]{:S(2)}, u32[]{:S(2)}) collective-permute-start(bf16[8,2,16,512]{3,2,1,0:T(8,128)(2,1)S(1)} %multiply_convert_fusion), channel_id=1, source_target_pairs={{0,32},{32,0},{64,96},{96,64},{128,160},{160,128},{192,224},{224,1... | collective-permute-start | bytes 786440 | tf_op jit(solution)/shard_map/ppermute | solution.py:12
  8.9 15.9 %collective-permute-start.3 = (bf16[8,2,16,512]{3,2,1,0:T(8,128)(2,1)S(1)}, bf16[8,2,16,512]{3,2,1,0:T(8,128)(2,1)S(1)}, u32[]{:S(2)}, u32[]{:S(2)}) collective-permute-start(bf16[8,2,16,512]{3,2,1,0:T(8,128)(2,1)S(1)} %get-tuple-element.6), channel_id=1, source_target_pairs={{0,64},{32,96},{64,0},{96,32},{128,192},{160,224},{192,128},{224,1... | collective-permute-start | bytes 786440 | tf_op jit(solution)/shard_map/ppermute | solution.py:12
  24.9 18.5 %collective-permute-start.4 = (bf16[8,2,16,512]{3,2,1,0:T(8,128)(2,1)S(1)}, bf16[8,2,16,512]{3,2,1,0:T(8,128)(2,1)S(1)}, u32[]{:S(2)}, u32[]{:S(2)}) collective-permute-start(bf16[8,2,16,512]{3,2,1,0:T(8,128)(2,1)S(1)} %broadcast_select_fusion.1), channel_id=1, source_target_pairs={{0,128},{32,160},{64,192},{96,224},{128,0},{160,32},{192,64},{224,... | collective-permute-start | bytes 786440 | tf_op jit(solution)/shard_map/ppermute | solution.py:12
  47.7 135.4 %all-to-all-start.1 = ((bf16[32,8,2,16,512]{4,3,2,1,0:T(8,128)(2,1)}), bf16[32,8,2,16,512]{4,3,2,1,0:T(8,128)(2,1)}, u32[]{:S(2)}, u32[]{:S(2)}) async-start(bf16[32,8,2,16,512]{4,3,2,1,0:T(8,128)(2,1)} %stack.28), calls=%async_computation.1 | async-start | bytes 16777216 | tf_op jit(solution)/shard_map/all_to_all | solution.py:75
  55.3 104.8 %collective-permute-start.1 = (bf16[8,2,16,512]{3,2,1,0:T(8,128)(2,1)S(1)}, bf16[8,2,16,512]{3,2,1,0:T(8,128)(2,1)S(1)}, u32[]{:S(2)}, u32[]{:S(2)}) collective-permute-start(bf16[8,2,16,512]{3,2,1,0:T(8,128)(2,1)S(1)} %get-tuple-element.5), channel_id=1, source_target_pairs={{0,64},{32,96},{64,0},{96,32},{128,192},{160,224},{192,128},{224,1... | collective-permute-start | bytes 786440 | tf_op jit(solution)/shard_map/ppermute | solution.py:12
  160.1 23.0 %collective-permute-start.2 = (bf16[8,2,16,512]{3,2,1,0:T(8,128)(2,1)S(1)}, bf16[8,2,16,512]{3,2,1,0:T(8,128)(2,1)S(1)}, u32[]{:S(2)}, u32[]{:S(2)}) collective-permute-start(bf16[8,2,16,512]{3,2,1,0:T(8,128)(2,1)S(1)} %broadcast_select_fusion.4), channel_id=1, source_target_pairs={{0,128},{32,160},{64,192},{96,224},{128,0},{160,32},{192,64},{224,... | collective-permute-start | bytes 786440 | tf_op jit(solution)/shard_map/ppermute | solution.py:12
  187.5 21.1 %copy-start = (bf16[8,2,16,512]{3,2,1,0:T(8,128)(2,1)S(1)}, bf16[8,2,16,512]{3,2,1,0:T(8,128)(2,1)}, u32[]{:S(2)}) copy-start(bf16[8,2,16,512]{3,2,1,0:T(8,128)(2,1)} %param.2) | copy-start | bytes 786436
  187.5 141.1 %all-to-all-start = ((bf16[32,8,2,16,512]{4,3,2,1,0:T(8,128)(2,1)}), bf16[32,8,2,16,512]{4,3,2,1,0:T(8,128)(2,1)}, u32[]{:S(2)}, u32[]{:S(2)}) async-start(bf16[32,8,2,16,512]{4,3,2,1,0:T(8,128)(2,1)} %stack.21), calls=%async_computation | async-start | bytes 16777216 | tf_op jit(solution)/shard_map/all_to_all | solution.py:75
  360.4 5.0 %copy-start.1 = (bf16[512,256,2,8,1]{1,3,4,2,0:T(8,128)(2,1)S(1)}, bf16[512,256,2,8,1]{1,3,4,2,0:T(8,128)(2,1)}, u32[]{:S(2)}) copy-start(bf16[512,256,2,8,1]{1,3,4,2,0:T(8,128)(2,1)} %fusion.32) | copy-start | bytes 12582916
